TPU v7x, 32 devices: a whole 2x2x4 slice. The times are simulated.
32 devices in a mesh: tier: 8 (over z, y), mat: 4 (over x, core).
Axes of the slice: x: 2, y: 2, z: 4, core: 2. Of those that a mesh axis runs over, the one named last changes fastest.
Arguments:
- costate: bfloat16 [128, 2, 256, 256], P(('tier', 'mat')), may hold values from -6 to 6
- hamiltonian: bfloat16 [256, 256], replicated, may hold values from -0.375 to 0.375
- couplers: bfloat16 [3, 256, 256], replicated, may hold values from -0.375 to 0.375
- damping: float32 [12], replicated, may hold values from 0.05 to 0.5
- coupling: float32 [2, 12], replicated, may hold values from -0.9 to 0.9
- levels: int32 [128, 12], P(('tier', 'mat')), may hold values from 0 to 3
- neighbour_slot: int32 [128, 24], P(('tier', 'mat')), may hold values from 0 to 15
- neighbour_mode: int32 [128, 24], P(('tier', 'mat')), may hold values from 0 to 11
- neighbour_flag: int32 [128, 24], P(('tier', 'mat')), may hold values from -1 to 1
- send_index: int32 [32, 16], P(('tier', 'mat')), may hold values from 0 to 3
Outputs:
- increment: float32 [128, 2, 256, 256], P(('tier', 'mat'))
- bath_gradient: float32 [12], replicated
All inputs are finite; a program needn't handle non-finite values.
Results may differ from a plain program's by a relative error of at most 0.0053.
Values may be sent and summed in bfloat16 or wider, within the bound.
A program may use at most 128 MiB of HBM per device.

v0:
```python
import functools

import jax
import jax.numpy as jnp
from jax import lax
from jax.experimental import pallas as pl
from jax.experimental.pallas import tpu as pltpu
from jax.sharding import PartitionSpec as P

ROWS = 16
F32 = jnp.float32
BF16 = jnp.bfloat16


def symmetric(weight):
    square = weight.astype(F32)
    return ((square + jnp.swapaxes(square, -1, -2)) * 0.5).astype(BF16)


def coefficients(coupling, levels, slot, mode, flag, slots):
    modes = levels.shape[1]
    mode_hot = mode[:, :, None] == jnp.arange(modes)[None, None, :]

    def pick(values):
        return jnp.sum(jnp.where(mode_hot, values, 0.0), -1)

    live = (flag >= 0).astype(F32)
    weight = jnp.sqrt(1.0 + pick(levels.astype(F32)[:, None, :])) * live
    real = pick(coupling[0][None, None, :]) * weight
    imag = pick(coupling[1][None, None, :]) * weight
    other = jnp.where(flag == 1, imag, -imag)
    op_hot = mode[:, :, None] % 3 == jnp.arange(3)[None, None, :]
    slot_hot = slot[:, :, None] == jnp.arange(slots)[None, None, :]
    both = op_hot[:, :, :, None] & slot_hot[:, :, None, :]

    def spread(values):
        return jnp.sum(jnp.where(both, values[:, :, None, None], 0.0), 1)

    creal, left, right = spread(real), spread(imag), spread(other)

    def parts(cimag):
        return jnp.stack([jnp.stack([creal, -cimag], -1), jnp.stack([cimag, creal], -1)], 1)

    table = jnp.stack([parts(left), parts(right)], 1)
    table = table.reshape(-1, slots * 2).astype(BF16)
    pair = mode_hot[:, :, :, None] & slot_hot[:, :, None, :]
    corr = jnp.sum(jnp.where(pair, weight[:, :, None, None], 0.0), 1)
    return table, corr


def blown_up(table):
    tall, wide = table.shape
    down = (jnp.arange(tall * ROWS)[:, None] // ROWS == jnp.arange(tall)[None, :]).astype(BF16)
    along = (jnp.arange(wide)[:, None] == jnp.arange(wide * ROWS)[None, :] // ROWS).astype(BF16)
    big = jnp.dot(down, table, preferred_element_type=F32).astype(BF16)
    big = jnp.dot(big, along, preferred_element_type=F32)
    keep = jnp.arange(tall * ROWS)[:, None] % ROWS == jnp.arange(wide * ROWS)[None, :] % ROWS
    return jnp.where(keep, big, 0.0).astype(BF16)


def section_kernel(first, decay_ref, coef_ref, state_ref, recv_ref, ops_ref, before_ref, out_ref, corr_ref, mixed):
    count, _, width, _ = state_ref.shape
    slots = recv_ref.shape[0]
    corr_ref[...] = before_ref[...]

    @pl.loop(0, width // ROWS)
    def _(step):
        rows = pl.ds(pl.multiple_of(step * ROWS, ROWS), ROWS)
        chunk = recv_ref[:, :, rows, :]
        sums = jnp.dot(
            coef_ref[...], chunk.reshape(slots * 2 * ROWS, width), preferred_element_type=F32
        ).astype(BF16)
        mixed[:, :, :, :, rows, :] = sums.reshape(count, 2, 2, 3, ROWS, width)
        for part in range(2):
            corr_ref[...] += lax.dot_general(
                state_ref[:, part, rows, :].reshape(count * ROWS, width),
                chunk[:, part].reshape(slots * ROWS, width),
                (((1,), (1,)), ((), ())),
                preferred_element_type=F32,
            )

    @pl.loop(0, count)
    def _(n):
        decay = decay_ref[n]
        for part in range(2):
            turned = -state_ref[n, 1] if part == 0 else state_ref[n, 0]
            rate = jnp.dot(ops_ref[0], turned, preferred_element_type=F32)
            for q in range(3):
                rate += jnp.dot(ops_ref[1 + q], mixed[n, 0, part, q], preferred_element_type=F32)
            back = jnp.dot(turned, ops_ref[0], preferred_element_type=F32)
            for q in range(3):
                back += jnp.dot(mixed[n, 1, part, q], ops_ref[1 + q], preferred_element_type=F32)
            own = state_ref[n, part].astype(F32)
            rate = rate - back - decay * own
            if first:
                out_ref[n, part] = (own + 0.125 * rate).astype(BF16)
            else:
                out_ref[n, part] = 0.25 * rate


def section(first, decay, coef, state, received, operators, before):
    count, _, width, _ = state.shape
    vmem = pl.BlockSpec(memory_space=pltpu.VMEM)
    return pl.pallas_call(
        functools.partial(section_kernel, first),
        out_shape=(
            jax.ShapeDtypeStruct(state.shape, BF16 if first else F32),
            jax.ShapeDtypeStruct(before.shape, F32),
        ),
        in_specs=[pl.BlockSpec(memory_space=pltpu.SMEM)] + [vmem] * 5,
        out_specs=(vmem, vmem),
        scratch_shapes=[pltpu.VMEM((count, 2, 2, 3, width, width), BF16)],
        compiler_params=pltpu.CompilerParams(vmem_limit_bytes=48 << 20),
        name="section_first" if first else "section_second",
    )(decay, coef, state, received, operators, before)


def receive(outgoing):
    return lax.all_to_all(outgoing, "tier", split_axis=0, concat_axis=0, tiled=True)


def per_device(
    costate,
    hamiltonian,
    couplers,
    damping,
    coupling,
    levels,
    neighbour_slot,
    neighbour_mode,
    neighbour_flag,
    send_index,
):
    count, _, width, _ = costate.shape
    slots = send_index.shape[1]
    received = receive(costate[send_index[0]])
    operators = jnp.concatenate([symmetric(hamiltonian)[None], symmetric(couplers)], 0)
    table, corr_weight = coefficients(
        coupling, levels, neighbour_slot, neighbour_mode, neighbour_flag, slots
    )
    coef = blown_up(table)
    decay = jnp.sum(levels.astype(F32) * damping[None, :], 1)
    corr = jnp.zeros((count * ROWS, slots * ROWS), F32)
    middle, corr = section(True, decay, coef, costate, received, operators, corr)
    received = receive(middle[send_index[0]])
    increment, corr = section(False, decay, coef, middle, received, operators, corr)
    row = jnp.arange(count * ROWS)[:, None]
    column = jnp.arange(slots * ROWS)[None, :]
    corr = jnp.where(row % ROWS == column % ROWS, corr, 0.0)
    pairs = jnp.sum(corr.reshape(count, ROWS, slots, ROWS), (1, 3)) / width
    grads = jnp.sum(pairs[:, None, :] * corr_weight, (0, 2))
    return increment, lax.psum(grads, ("tier", "mat"))


def solution(mesh):
    blocks = P(("tier", "mat"), None)
    return jax.shard_map(
        per_device,
        mesh=mesh,
        in_specs=(P(("tier", "mat"), None, None, None), P(), P(), P(), P()) + (blocks,) * 5,
        out_specs=(P(("tier", "mat"), None, None, None), P()),
        check_vma=False,
    )
```

profile of v0, /device:TPU:0, one launch (start us, length us, event | category | flops | bytes accessed | tf_op | source)
XLA Modules:
  0.0 269.3 jit_solution(10185686726492980066)
XLA Ops:
  0.6 0.7 fusion.27
  1.3 4.0 %gather_fusion = bf16[16,2,256,256]{3,2,1,0:T(8,128)(2,1)} fusion(bf16[4,2,256,256]{3,2,1,0:T(8,128)(2,1)} %state_ref.1, s32[1024]{0:T(1024)S(1)} %pad_clamp_fusion), kind=kCustom, calls=%fused_computation | custom fusion | bytes 8388672 | tf_op jit(solution)/shard_map/gather | solution.py:136
  5.3 0.0 copy-start.5
  5.3 0.0 copy-start.7
  5.3 0.0 copy-start.3
  5.3 0.0 copy-start.6
  5.3 0.0 copy-start.4
  5.3 0.0 copy-start.1
  5.3 0.0 copy-start.2
  5.4 0.0 copy-start.8
  5.4 7.5 %all-to-all-start = ((bf16[16,2,256,256]{3,2,1,0:T(8,128)(2,1)}), bf16[16,2,256,256]{3,2,1,0:T(8,128)(2,1)}, u32[]{:S(2)}, u32[]{:S(2)}) async-start(bf16[16,2,256,256]{3,2,1,0:T(8,128)(2,1)} %gather_fusion), calls=%async_computation | async-start | bytes 8388608 | tf_op jit(solution)/shard_map/all_to_all | solution.py:119
  12.8 0.0 copy-done.5
  12.8 0.0 copy-start
  12.8 0.1 copy.32
  12.9 0.0 copy-done.7
  12.9 0.0 copy-done.3
  13.0 0.1 select_reduce_fusion.1
  13.1 0.0 copy-done.6
  13.1 0.0 copy-done.4
  13.2 0.2 fusion.8
  13.5 0.3 copy.35
  13.8 0.2 convert_element_type.30
  14.0 0.0 copy-done.1
  14.0 0.2 copy.38
  14.2 0.2 copy.39
  14.3 0.0 copy-done.2
  14.3 0.1 copy.36
  14.5 0.1 copy.37
  14.6 0.0 copy-done.8
  14.6 0.1 multiply_reduce_fusion.1.decay_ref
  14.7 0.1 fusion.1
  14.9 0.6 select_convert_fusion.coef_ref
  15.6 90.5 %all-to-all-done.recv_ref = bf16[16,2,256,256]{3,2,1,0:T(8,128)(2,1)} async-done(((bf16[16,2,256,256]{3,2,1,0:T(8,128)(2,1)}), bf16[16,2,256,256]{3,2,1,0:T(8,128)(2,1)}, u32[]{:S(2)}, u32[]{:S(2)}) %all-to-all-start) | async-done | bytes 4194336 | tf_op jit(solution)/shard_map/all_to_all | solution.py:119
  106.1 0.0 copy-done
  106.1 11.9 %section_first.1 = (bf16[4,2,256,256]{3,2,1,0:T(8,128)(2,1)S(1)}, f32[64,256]{1,0:T(8,128)S(1)}) custom-call(f32[4]{0:T(128)S(1)} %multiply_reduce_fusion.1.decay_ref, bf16[768,512]{1,0:T(8,128)(2,1)S(1)} %select_convert_fusion.coef_ref, bf16[4,2,256,256]{3,2,1,0:T(8,128)(2,1)S(1)} %copy-done, bf16[16,2,256,256]{3,2,1,0:T(8,128)(2,1)} %all-to-all-done.recv_ref, ...), custom_call_target="tpu_custom_call" | custom-call | tf_op jit(solution)/shard_map/section_first/pallas_call | solution.py:104
  118.0 2.8 %gather_fusion.1 = bf16[16,2,256,256]{3,2,1,0:T(8,128)(2,1)} fusion(bf16[4,2,256,256]{3,2,1,0:T(8,128)(2,1)S(1)} %get-tuple-element.6.state_ref, s32[1024]{0:T(1024)S(1)} %pad_clamp_fusion), kind=kCustom, calls=%fused_computation.1 | custom fusion | bytes 8388672 | tf_op jit(solution)/shard_map/gather | solution.py:145
  120.8 4.5 %all-to-all-start.1 = ((bf16[16,2,256,256]{3,2,1,0:T(8,128)(2,1)}), bf16[16,2,256,256]{3,2,1,0:T(8,128)(2,1)}, u32[]{:S(2)}, u32[]{:S(2)}) async-start(bf16[16,2,256,256]{3,2,1,0:T(8,128)(2,1)} %gather_fusion.1), calls=%async_computation.1 | async-start | bytes 8388608 | tf_op jit(solution)/shard_map/all_to_all | solution.py:119
  125.4 0.2 select_reduce_fusion
  125.6 92.3 %all-to-all-done.1.recv_ref = bf16[16,2,256,256]{3,2,1,0:T(8,128)(2,1)} async-done(((bf16[16,2,256,256]{3,2,1,0:T(8,128)(2,1)}), bf16[16,2,256,256]{3,2,1,0:T(8,128)(2,1)}, u32[]{:S(2)}, u32[]{:S(2)}) %all-to-all-start.1) | async-done | bytes 4194336 | tf_op jit(solution)/shard_map/all_to_all | solution.py:119
  217.9 13.2 %section_second.1 = (f32[4,2,256,256]{3,2,1,0:T(8,128)}, f32[64,256]{1,0:T(8,128)S(1)}) custom-call(f32[4]{0:T(128)S(1)} %multiply_reduce_fusion.1.decay_ref, bf16[768,512]{1,0:T(8,128)(2,1)S(1)} %select_convert_fusion.coef_ref, bf16[4,2,256,256]{3,2,1,0:T(8,128)(2,1)S(1)} %get-tuple-element.6.state_ref, bf16[16,2,256,256]{3,2,1,0:T(8,128)(2,1)} %all-to-all-done.1.recv_ref, ...), custom_call_target="tpu_custom_call" | custom-call | tf_op jit(solution)/shard_map/section_second/pallas_call | solution.py:104
  231.1 0.1 compare_select_fusion
  231.1 0.2 reshape.214
  231.3 0.1 reduce_sum.103
  231.5 0.1 multiply_reduce_fusion
  231.6 37.8 %psum.7 = f32[12]{0:T(128)} all-reduce(f32[12]{0:T(128)S(1)} %multiply_reduce_fusion), channel_id=1, replica_groups=mesh['tier'=8,'mat'=4] {'tier','mat'}, use_global_device_ids=true, to_apply=%region_10.11 | all-reduce | flops 12 | bytes 96 | tf_op jit(solution)/shard_map/psum | solution.py:152
  (23 shorter events, 0.3 us)
Async XLA Ops:
  5.3 7.5 %copy-start.5 = (s32[4,12]{1,0:T(4,128)S(1)}, s32[4,12]{1,0:T(4,128)}, u32[]{:S(2)}) copy-start(s32[4,12]{1,0:T(4,128)} %param.15) | copy-start | bytes 580
  5.3 7.6 %copy-start.7 = (f32[2,12]{1,0:T(2,128)S(1)}, f32[2,12]{1,0:T(2,128)}, u32[]{:S(2)}) copy-start(f32[2,12]{1,0:T(2,128)} %param.14) | copy-start | bytes 292
  5.3 7.6 %copy-start.3 = (s32[4,24]{1,0:T(4,128)S(1)}, s32[4,24]{1,0:T(4,128)}, u32[]{:S(2)}) copy-start(s32[4,24]{1,0:T(4,128)} %param.17) | copy-start | bytes 1156
  5.3 7.8 %copy-start.6 = (s32[4,24]{1,0:T(4,128)S(1)}, s32[4,24]{1,0:T(4,128)}, u32[]{:S(2)}) copy-start(s32[4,24]{1,0:T(4,128)} %param.16) | copy-start | bytes 1156
  5.3 7.8 %copy-start.4 = (s32[4,24]{1,0:T(4,128)S(1)}, s32[4,24]{1,0:T(4,128)}, u32[]{:S(2)}) copy-start(s32[4,24]{1,0:T(4,128)} %param.18) | copy-start | bytes 1156
  5.3 8.7 %copy-start.1 = (bf16[3,256,256]{2,1,0:T(8,128)(2,1)S(1)}, bf16[3,256,256]{2,1,0:T(8,128)(2,1)}, u32[]{:S(2)}) copy-start(bf16[3,256,256]{2,1,0:T(8,128)(2,1)} %param.12) | copy-start | bytes 1179652
  5.3 9.0 %copy-start.2 = (bf16[256,256]{1,0:T(8,128)(2,1)S(1)}, bf16[256,256]{1,0:T(8,128)(2,1)}, u32[]{:S(2)}) copy-start(bf16[256,256]{1,0:T(8,128)(2,1)} %param.11) | copy-start | bytes 393220
  5.4 9.2 %copy-start.8 = (f32[12]{0:T(128)S(1)}, f32[12]{0:T(128)}, u32[]{:S(2)}) copy-start(f32[12]{0:T(128)} %param.13) | copy-start | bytes 148
  5.4 100.7 %all-to-all-start = ((bf16[16,2,256,256]{3,2,1,0:T(8,128)(2,1)}), bf16[16,2,256,256]{3,2,1,0:T(8,128)(2,1)}, u32[]{:S(2)}, u32[]{:S(2)}) async-start(bf16[16,2,256,256]{3,2,1,0:T(8,128)(2,1)} %gather_fusion), calls=%async_computation | async-start | bytes 8388608 | tf_op jit(solution)/shard_map/all_to_all | solution.py:119
  12.8 93.3 %copy-start = (bf16[4,2,256,256]{3,2,1,0:T(8,128)(2,1)S(1)}, bf16[4,2,256,256]{3,2,1,0:T(8,128)(2,1)}, u32[]{:S(2)}) copy-start(bf16[4,2,256,256]{3,2,1,0:T(8,128)(2,1)} %state_ref.1) | copy-start | bytes 3145732
  120.8 97.1 %all-to-all-start.1 = ((bf16[16,2,256,256]{3,2,1,0:T(8,128)(2,1)}), bf16[16,2,256,256]{3,2,1,0:T(8,128)(2,1)}, u32[]{:S(2)}, u32[]{:S(2)}) async-start(bf16[16,2,256,256]{3,2,1,0:T(8,128)(2,1)} %gather_fusion.1), calls=%async_computation.1 | async-start | bytes 8388608 | tf_op jit(solution)/shard_map/all_to_all | solution.py:119
where the time goes:
time: 271 us; the launch traced here: 269 us
  waiting for transfers between devices  183 us (68%)
  blocking collectives  37.8 us (14%)
  Pallas kernels  25 us (9%)
  starting transfers between devices  12 us (4%)
  local copies, waits for them, and re-layouts  8.17 us (3%)
    all_to_all x2, waiting for transfers between devices, receive(): lax.all_to_all(outgoing, 'tier', split_axis=0, concat_axis=0, tiled=True)  183 us
    psum x1, blocking collectives, per_device(): return (increment, lax.psum(grads, ('tier', 'mat')))  37.8 us
    pallas_call x2, Pallas kernels, section(): pl.pallas_call(functools.partial(section_kernel, first), out_shape=(jax.S...  25 us
    all_to_all x2, starting transfers between devices, receive(): lax.all_to_all(outgoing, 'tier', split_axis=0, concat_axis=0, tiled=True)  12 us
  transfers between devices with their start and end apart: 2, of which 2 were waited for; matrix products, arithmetic and copies ran while one was open for 1% of the time, Pallas kernels for 0%

commit v1 on v0

--- a/solution.py
+++ b/solution.py
@@ -10,6 +10,7 @@
 ROWS = 16
 F32 = jnp.float32
 BF16 = jnp.bfloat16
+MESH = pl.DeviceIdType.MESH
 
 
 def symmetric(weight):
@@ -42,10 +43,12 @@
         return jnp.stack([jnp.stack([creal, -cimag], -1), jnp.stack([cimag, creal], -1)], 1)
 
     table = jnp.stack([parts(left), parts(right)], 1)
-    table = table.reshape(-1, slots * 2).astype(BF16)
+    table = table.reshape(-1, slots * 2)
+    table_high = table.astype(BF16)
+    table_low = (table - table_high.astype(F32)).astype(BF16)
     pair = mode_hot[:, :, :, None] & slot_hot[:, :, None, :]
     corr = jnp.sum(jnp.where(pair, weight[:, :, None, None], 0.0), 1)
-    return table, corr
+    return table_high, table_low, corr
 
 
 def blown_up(table):
@@ -58,18 +61,19 @@
     return jnp.where(keep, big, 0.0).astype(BF16)
 
 
-def section_kernel(first, decay_ref, coef_ref, state_ref, recv_ref, ops_ref, before_ref, out_ref, corr_ref, mixed):
+def section_kernel(first, decay_ref, coef_ref, state_ref, near_ref, far_ref, ops_ref, before_ref, out_ref, corr_ref, mixed):
     count, _, width, _ = state_ref.shape
-    slots = recv_ref.shape[0]
+    slots = near_ref.shape[0] + far_ref.shape[0]
     corr_ref[...] = before_ref[...]
 
     @pl.loop(0, width // ROWS)
     def _(step):
         rows = pl.ds(pl.multiple_of(step * ROWS, ROWS), ROWS)
-        chunk = recv_ref[:, :, rows, :]
-        sums = jnp.dot(
-            coef_ref[...], chunk.reshape(slots * 2 * ROWS, width), preferred_element_type=F32
-        ).astype(BF16)
+        chunk = jnp.concatenate([near_ref[:, :, rows, :], far_ref[:, :, rows, :]], 0)
+        tall = chunk.reshape(slots * 2 * ROWS, width)
+        sums = jnp.dot(coef_ref[0], tall, preferred_element_type=F32)
+        sums += jnp.dot(coef_ref[1], tall, preferred_element_type=F32)
+        sums = sums.astype(BF16)
         mixed[:, :, :, :, rows, :] = sums.reshape(count, 2, 2, 3, ROWS, width)
         for part in range(2):
             corr_ref[...] += lax.dot_general(
@@ -98,7 +102,7 @@
                 out_ref[n, part] = 0.25 * rate
 
 
-def section(first, decay, coef, state, received, operators, before):
+def section(first, decay, coef, state, near, far, operators, before):
     count, _, width, _ = state.shape
     vmem = pl.BlockSpec(memory_space=pltpu.VMEM)
     return pl.pallas_call(
@@ -107,19 +111,132 @@
             jax.ShapeDtypeStruct(state.shape, BF16 if first else F32),
             jax.ShapeDtypeStruct(before.shape, F32),
         ),
-        in_specs=[pl.BlockSpec(memory_space=pltpu.SMEM)] + [vmem] * 5,
+        in_specs=[pl.BlockSpec(memory_space=pltpu.SMEM)] + [vmem] * 6,
         out_specs=(vmem, vmem),
         scratch_shapes=[pltpu.VMEM((count, 2, 2, 3, width, width), BF16)],
         compiler_params=pltpu.CompilerParams(vmem_limit_bytes=48 << 20),
         name="section_first" if first else "section_second",
-    )(decay, coef, state, received, operators, before)
-
-
-def receive(outgoing):
-    return lax.all_to_all(outgoing, "tier", split_axis=0, concat_axis=0, tiled=True)
+    )(decay, coef, state, near, far, operators, before)
+
+
+def greet(devices):
+    barrier = pltpu.get_barrier_semaphore()
+    for device in devices:
+        pl.semaphore_signal(barrier, inc=1, device_id=device, device_id_type=MESH)
+    pl.semaphore_wait(barrier, len(devices))
+
+
+def remote(source, target, send, landed, device):
+    return pltpu.make_async_remote_copy(
+        src_ref=source,
+        dst_ref=target,
+        send_sem=send,
+        recv_sem=landed,
+        device_id=device,
+        device_id_type=MESH,
+    )
+
+
+def exchange_kernel(tiers, whole, *refs):
+    if whole:
+        out_ref, state_ref, index_ref, near_ref, block_ref, other_ref, send, landed, own = refs
+    else:
+        out_ref, near_ref, send, landed, own = refs
+    half = tiers // 2
+    me, mat = lax.axis_index("tier"), lax.axis_index("mat")
+    base = me // half * half
+    local = me - base
+    peers = [lax.rem(local + d, half) for d in range(1, half)]
+    partner = (lax.rem(me + half, tiers), mat)
+    greet([(base + peer, mat) for peer in peers] + ([partner] if whole else []))
+    copies = []
+    if whole:
+        copies.append(remote(state_ref, block_ref, send.at[0], landed.at[0], partner))
+        copies.append(remote(index_ref, other_ref, send.at[half], landed.at[half], partner))
+    for d, peer in enumerate(peers, 1):
+        copies.append(
+            remote(out_ref.at[peer], near_ref.at[local], send.at[d], landed.at[d], (base + peer, mat))
+        )
+    keep = pltpu.make_async_copy(out_ref.at[local], near_ref.at[local], own)
+    for copy in copies:
+        copy.start()
+    keep.start()
+    for copy in copies:
+        copy.wait()
+    keep.wait()
+
+
+def exchange(tiers, number, out, state=None, index=None):
+    whole = state is not None
+    args = (out, state, index) if whole else (out,)
+    anywhere = pl.BlockSpec(memory_space=pl.ANY)
+    half = tiers // 2
+    return pl.pallas_call(
+        functools.partial(exchange_kernel, tiers, whole),
+        out_shape=tuple(jax.ShapeDtypeStruct(a.shape, a.dtype) for a in args),
+        in_specs=[anywhere] * len(args),
+        out_specs=(anywhere,) * len(args),
+        scratch_shapes=[
+            pltpu.SemaphoreType.DMA((half + 1,)),
+            pltpu.SemaphoreType.DMA((half + 1,)),
+            pltpu.SemaphoreType.DMA,
+        ],
+        compiler_params=pltpu.CompilerParams(collective_id=number, has_side_effects=True),
+        name="exchange_whole" if whole else "exchange_half",
+    )(*args)
+
+
+def total_kernel(tiers, mats, value_ref, total_ref, by_tier, by_mat, middle, send, landed, send_mat, landed_mat):
+    me, mat = lax.axis_index("tier"), lax.axis_index("mat")
+    along = [(lax.rem(me + d, tiers), mat) for d in range(1, tiers)]
+    across = [(me, lax.rem(mat + d, mats)) for d in range(1, mats)]
+    greet(along + across)
+    copies = [
+        remote(value_ref, by_tier.at[me], send.at[d], landed.at[d], device)
+        for d, device in enumerate(along)
+    ]
+    for copy in copies:
+        copy.start()
+    by_tier[me] = value_ref[...]
+    for copy in copies:
+        copy.wait()
+    middle[...] = jnp.sum(by_tier[...], 0)
+    by_mat[mat] = middle[...]
+    copies = [
+        remote(middle, by_mat.at[mat], send_mat.at[d], landed_mat.at[d], device)
+        for d, device in enumerate(across)
+    ]
+    for copy in copies:
+        copy.start()
+    for copy in copies:
+        copy.wait()
+    total_ref[...] = jnp.sum(by_mat[...], 0)
+
+
+def total(tiers, mats, number, value):
+    vmem = pl.BlockSpec(memory_space=pltpu.VMEM)
+    return pl.pallas_call(
+        functools.partial(total_kernel, tiers, mats),
+        out_shape=jax.ShapeDtypeStruct(value.shape, F32),
+        in_specs=[vmem],
+        out_specs=vmem,
+        scratch_shapes=[
+            pltpu.VMEM((tiers,) + value.shape, F32),
+            pltpu.VMEM((mats,) + value.shape, F32),
+            pltpu.VMEM(value.shape, F32),
+            pltpu.SemaphoreType.DMA((tiers - 1,)),
+            pltpu.SemaphoreType.DMA((tiers - 1,)),
+            pltpu.SemaphoreType.DMA((mats - 1,)),
+            pltpu.SemaphoreType.DMA((mats - 1,)),
+        ],
+        compiler_params=pltpu.CompilerParams(collective_id=number, has_side_effects=True),
+        name="total",
+    )(value)
 
 
 def per_device(
+    tiers,
+    mats,
     costate,
     hamiltonian,
     couplers,
@@ -133,29 +250,46 @@
 ):
     count, _, width, _ = costate.shape
     slots = send_index.shape[1]
-    received = receive(costate[send_index[0]])
+    half, cap = tiers // 2, slots // tiers
+    me = lax.axis_index("tier")
+    base = me // half * half
+
+    def chosen(state, index):
+        mine = lax.dynamic_slice(index[0], (base * cap,), (half * cap,))
+        return state[mine].reshape((half, cap) + state.shape[1:])
+
+    def flat(received):
+        return received.reshape((half * cap,) + received.shape[2:])
+
+    out = chosen(costate, send_index)
+    near, block, other_index = exchange(tiers, 0, out, costate, send_index)
+    (far,) = exchange(tiers, 1, chosen(block, other_index))
     operators = jnp.concatenate([symmetric(hamiltonian)[None], symmetric(couplers)], 0)
-    table, corr_weight = coefficients(
-        coupling, levels, neighbour_slot, neighbour_mode, neighbour_flag, slots
+    nearest = (neighbour_slot + base * cap) % slots
+    table_high, table_low, corr_weight = coefficients(
+        coupling, levels, nearest, neighbour_mode, neighbour_flag, slots
     )
-    coef = blown_up(table)
+    coef = jnp.stack([blown_up(table_high), blown_up(table_low)])
     decay = jnp.sum(levels.astype(F32) * damping[None, :], 1)
     corr = jnp.zeros((count * ROWS, slots * ROWS), F32)
-    middle, corr = section(True, decay, coef, costate, received, operators, corr)
-    received = receive(middle[send_index[0]])
-    increment, corr = section(False, decay, coef, middle, received, operators, corr)
+    middle, corr = section(True, decay, coef, costate, flat(near), flat(far), operators, corr)
+    near, block, _ = exchange(tiers, 2, chosen(middle, send_index), middle, send_index)
+    (far,) = exchange(tiers, 3, chosen(block, other_index))
+    increment, corr = section(False, decay, coef, middle, flat(near), flat(far), operators, corr)
     row = jnp.arange(count * ROWS)[:, None]
     column = jnp.arange(slots * ROWS)[None, :]
     corr = jnp.where(row % ROWS == column % ROWS, corr, 0.0)
     pairs = jnp.sum(corr.reshape(count, ROWS, slots, ROWS), (1, 3)) / width
     grads = jnp.sum(pairs[:, None, :] * corr_weight, (0, 2))
-    return increment, lax.psum(grads, ("tier", "mat"))
+    modes = grads.shape[0]
+    padded = jnp.zeros((8, 128), F32).at[0, :modes].set(grads)
+    return increment, total(tiers, mats, 4, padded)[0, :modes]
 
 
 def solution(mesh):
     blocks = P(("tier", "mat"), None)
     return jax.shard_map(
-        per_device,
+        functools.partial(per_device, mesh.shape["tier"], mesh.shape["mat"]),
         mesh=mesh,
         in_specs=(P(("tier", "mat"), None, None, None), P(), P(), P(), P()) + (blocks,) * 5,
         out_specs=(P(("tier", "mat"), None, None, None), P()),

time: 271 us -> 219 us (0.81)
  waiting for transfers between devices: 183 us -> 0 us
  Pallas kernels: 25 us -> 194 us
  blocking collectives: 37.8 us -> 0 us
  starting transfers between devices: 12 us -> 0 us
  local copies, waits for them, and re-layouts: 8.17 us -> 18.8 us
    all_to_all x2 -> x0, waiting for transfers between devices: 183 us -> none  [receive(): lax.all_to_all(outgoing, 'tier', split_axis=0, concat_axis=0, tiled=True)]
    pallas_call x0 -> x5, Pallas kernels: none -> 162 us  [the longest x4 151 us: exchange(): pl.pallas_call(functools.partial(exchange_kernel, tiers, whole), out_shap...]
    psum x1 -> x0, blocking collectives: 37.8 us -> none  [per_device(): return (increment, lax.psum(grads, ('tier', 'mat')))]
    all_to_all x2 -> x0, starting transfers between devices: 12 us -> none  [receive(): lax.all_to_all(outgoing, 'tier', split_axis=0, concat_axis=0, tiled=True)]
    pallas_call x2, Pallas kernels: 25 us -> 31.2 us  [section(): pl.pallas_call(functools.partial(section_kernel, first), out_shape=(jax.S...]
    gather x2 -> x4, local copies, waits for them, and re-layouts: 6.79 us -> 11.7 us  [chosen(): return state[mine].reshape((half, cap) + state.shape[1:])]
    unnamed x20 -> x30, local copies, waits for them, and re-layouts: 0.32 us -> 3.98 us
  transfers between devices with their start and end apart: 2 -> 0, of which waited for: 2 -> 0; matrix products, arithmetic and copies ran while one was open for 1% -> 0% of each run, Pallas kernels for 0% -> 0%
where the time goes in v1:
time: 219 us
  Pallas kernels  194 us (89%)
  local copies, waits for them, and re-layouts  18.8 us (9%)
  other arithmetic  3.97 us (2%)
    pallas_call x4, Pallas kernels, exchange(): pl.pallas_call(functools.partial(exchange_kernel, tiers, whole), out_shap...  151 us
    pallas_call x2, Pallas kernels, section(): pl.pallas_call(functools.partial(section_kernel, first), out_shape=(jax.S...  31.2 us
    gather x4, local copies, waits for them, and re-layouts, chosen(): return state[mine].reshape((half, cap) + state.shape[1:])  11.7 us
    pallas_call x1, Pallas kernels, total(): pl.pallas_call(functools.partial(total_kernel, tiers, mats), out_shape=ja...  11 us

profile of v1, /device:TPU:0, one launch (start us, length us, event | category | flops | bytes accessed | tf_op | source)
XLA Modules:
  0.0 218.7 jit_solution(11633313382116688887)
XLA Ops:
  0.6 0.7 fusion.37
  1.4 3.2 %gather_fusion = bf16[8,2,256,256]{3,2,1,0:T(8,128)(2,1)} fusion(bf16[4,2,256,256]{3,2,1,0:T(8,128)(2,1)} %state_ref.1, s32[1024]{0:T(1024)S(1)} %pad_clamp_fusion.1), kind=kCustom, calls=%fused_computation | custom fusion | bytes 4194336 | tf_op jit(solution)/shard_map/gather | solution.py:259
  4.6 52.5 %exchange_whole.2 = (bf16[4,2,2,256,256]{4,3,2,1,0:T(8,128)(2,1)}, bf16[4,2,256,256]{3,2,1,0:T(8,128)(2,1)}, s32[1,16]{1,0:T(1,128)}) custom-call(bf16[4,2,2,256,256]{4,3,2,1,0:T(8,128)(2,1)} %bitcast.64, bf16[4,2,256,256]{3,2,1,0:T(8,128)(2,1)} %state_ref.1, s32[1,16]{1,0:T(1,128)} %refs_2_.3), custom_call_target="tpu_custom_call" | custom-call | tf_op jit(solution)/shard_map/exchange_whole/pallas_call | solution.py:174
  57.1 0.6 fusion.38
  57.7 3.2 %gather_fusion.1 = bf16[8,2,256,256]{3,2,1,0:T(8,128)(2,1)} fusion(bf16[4,2,256,256]{3,2,1,0:T(8,128)(2,1)} %get-tuple-element.24, s32[1024]{0:T(1024)S(1)} %pad_clamp_fusion), kind=kCustom, calls=%fused_computation.1 | custom fusion | bytes 4194336 | tf_op jit(solution)/shard_map/gather | solution.py:259
  61.0 0.0 copy-start.9
  61.0 25.4 %exchange_half.2 = bf16[4,2,2,256,256]{4,3,2,1,0:T(8,128)(2,1)} custom-call(bf16[4,2,2,256,256]{4,3,2,1,0:T(8,128)(2,1)} %bitcast.66), custom_call_target="tpu_custom_call" | custom-call | tf_op jit(solution)/shard_map/exchange_half/pallas_call | solution.py:174
  86.4 0.0 copy-done.11
  86.5 0.0 copy-done.12
  86.5 0.0 copy-done.10
  86.5 0.1 copy.27
  86.6 0.1 select_reduce_fusion.1
  86.8 0.2 fusion.14
  87.1 0.4 copy.36
  87.5 0.4 reshape.299
  87.9 0.6 fusion.3
  88.6 0.0 copy-start.6
  88.6 0.6 fusion.2
  89.2 1.3 pad_maximum_fusion.coef_ref
  90.5 0.2 copy.39
  90.7 0.2 copy.40
  90.9 0.0 copy-start.13
  90.9 0.0 copy-start
  90.9 0.1 fusion.5
  91.0 0.4 copy-done.7
  91.4 0.1 copy.37
  91.5 0.1 copy.38
  91.7 0.0 copy-done.13
  91.8 0.1 multiply_reduce_fusion.1.decay_ref
  91.9 0.3 copy-done
  92.1 1.4 copy-done.3
  93.5 15.2 %section_first.1 = (bf16[4,2,256,256]{3,2,1,0:T(8,128)(2,1)S(1)}, f32[64,256]{1,0:T(8,128)S(1)}) custom-call(f32[4]{0:T(128)S(1)} %multiply_reduce_fusion.1.decay_ref, bf16[2,768,512]{2,1,0:T(8,128)(2,1)S(1)} %copy-done.3, bf16[4,2,256,256]{3,2,1,0:T(8,128)(2,1)S(1)} %copy-done, bf16[8,2,256,256]{3,2,1,0:T(8,128)(2,1)} %bitcast.69, ...), custom_call_target="tpu_custom_call" | custom-call | tf_op jit(solution)/shard_map/section_first/pallas_call | solution.py:108
  108.8 0.0 copy-start.1
  108.8 2.0 gather_fusion.2
  110.8 0.0 copy-done.1
  110.8 48.9 %exchange_whole.3 = (bf16[4,2,2,256,256]{4,3,2,1,0:T(8,128)(2,1)}, bf16[4,2,256,256]{3,2,1,0:T(8,128)(2,1)}, s32[1,16]{1,0:T(1,128)}) custom-call(bf16[4,2,2,256,256]{4,3,2,1,0:T(8,128)(2,1)} %bitcast.63, bf16[4,2,256,256]{3,2,1,0:T(8,128)(2,1)} %copy-done.1, s32[1,16]{1,0:T(1,128)} %refs_2_.3), custom_call_target="tpu_custom_call" | custom-call | tf_op jit(solution)/shard_map/exchange_whole/pallas_call | solution.py:174
  159.7 3.2 %gather_fusion.3 = bf16[8,2,256,256]{3,2,1,0:T(8,128)(2,1)} fusion(bf16[4,2,256,256]{3,2,1,0:T(8,128)(2,1)} %get-tuple-element.28, s32[1024]{0:T(1024)S(1)} %pad_clamp_fusion), kind=kCustom, calls=%fused_computation.3 | custom fusion | bytes 4194336 | tf_op jit(solution)/shard_map/gather | solution.py:259
  162.9 24.7 %exchange_half.3 = bf16[4,2,2,256,256]{4,3,2,1,0:T(8,128)(2,1)} custom-call(bf16[4,2,2,256,256]{4,3,2,1,0:T(8,128)(2,1)} %bitcast.65), custom_call_target="tpu_custom_call" | custom-call | tf_op jit(solution)/shard_map/exchange_half/pallas_call | solution.py:174
  187.7 1.6 copy-done.5
  189.2 15.9 %section_second.1 = (f32[4,2,256,256]{3,2,1,0:T(8,128)}, f32[64,256]{1,0:T(8,128)S(1)}) custom-call(f32[4]{0:T(128)S(1)} %multiply_reduce_fusion.1.decay_ref, bf16[2,768,512]{2,1,0:T(8,128)(2,1)S(1)} %copy-done.4, bf16[4,2,256,256]{3,2,1,0:T(8,128)(2,1)S(1)} %copy-done.2, bf16[8,2,256,256]{3,2,1,0:T(8,128)(2,1)S(1)} %bitcast.62, ...), custom_call_target="tpu_custom_call" | custom-call | tf_op jit(solution)/shard_map/section_second/pallas_call | solution.py:108
  205.2 0.1 compare_select_fusion.2
  205.3 0.2 reshape.308
  205.5 0.1 reduce_sum.103
  205.6 0.2 select_reduce_fusion
  205.8 0.1 multiply_reduce_fusion
  205.9 0.6 scatter.4.value_ref
  206.5 11.0 %total.1 = f32[8,128]{1,0:T(8,128)} custom-call(f32[8,128]{1,0:T(8,128)} %scatter.4.value_ref), custom_call_target="tpu_custom_call" | custom-call | tf_op jit(solution)/shard_map/total/pallas_call | solution.py:218
  217.5 1.2 slice_bitcast_fusion
  (44 shorter events, 0.3 us)
Async XLA Ops:
  61.0 25.5 %copy-start.11 = (s32[4,24]{1,0:T(4,128)S(1)}, s32[4,24]{1,0:T(4,128)}, u32[]{:S(2)}) copy-start(s32[4,24]{1,0:T(4,128)} %param.18) | copy-start | bytes 1156
  61.0 25.5 %copy-start.12 = (f32[2,12]{1,0:T(2,128)S(1)}, f32[2,12]{1,0:T(2,128)}, u32[]{:S(2)}) copy-start(f32[2,12]{1,0:T(2,128)} %param.16) | copy-start | bytes 292
  61.0 25.5 %copy-start.10 = (s32[4,12]{1,0:T(4,128)S(1)}, s32[4,12]{1,0:T(4,128)}, u32[]{:S(2)}) copy-start(s32[4,12]{1,0:T(4,128)} %param.17) | copy-start | bytes 580
  61.0 25.6 %copy-start.8 = (s32[4,24]{1,0:T(4,128)S(1)}, s32[4,24]{1,0:T(4,128)}, u32[]{:S(2)}) copy-start(s32[4,24]{1,0:T(4,128)} %param.19) | copy-start | bytes 1156
  61.0 25.8 %copy-start.9 = (s32[4,24]{1,0:T(4,128)S(1)}, s32[4,24]{1,0:T(4,128)}, u32[]{:S(2)}) copy-start(s32[4,24]{1,0:T(4,128)} %param.20) | copy-start | bytes 1156
  88.6 2.0 copy-start.6
  90.5 0.9 copy-start.7
  90.9 0.9 copy-start.13
  90.9 1.2 copy-start
  92.1 1.4 copy-start.3
  108.8 2.0 copy-start.1
  162.9 24.7 %copy-start.2 = (bf16[4,2,256,256]{3,2,1,0:T(8,128)(2,1)S(1)}, bf16[4,2,256,256]{3,2,1,0:T(8,128)(2,1)}, u32[]{:S(2)}) copy-start(bf16[4,2,256,256]{3,2,1,0:T(8,128)(2,1)} %copy-done.1) | copy-start | bytes 3145732
  162.9 24.7 %copy-start.4 = (bf16[2,768,512]{2,1,0:T(8,128)(2,1)S(1)}, bf16[2,768,512]{2,1,0:T(8,128)(2,1)}, u32[]{:S(2)}) copy-start(bf16[2,768,512]{2,1,0:T(8,128)(2,1)} %pad_maximum_fusion.coef_ref) | copy-start | bytes 4718596
  187.6 1.6 copy-start.5

commit v2 on v1

v2 whole, which is shorter than its diff:
```python
import functools

import jax
import jax.numpy as jnp
from jax import lax
from jax.experimental import pallas as pl
from jax.experimental.pallas import tpu as pltpu
from jax.sharding import PartitionSpec as P

ROWS = 16
PIECES = 4
F32 = jnp.float32
BF16 = jnp.bfloat16
MESH = pl.DeviceIdType.MESH


def symmetric(weight):
    square = weight.astype(F32)
    return ((square + jnp.swapaxes(square, -1, -2)) * 0.5).astype(BF16)


def coefficients(coupling, levels, slot, mode, flag, slots):
    modes = levels.shape[1]
    mode_hot = mode[:, :, None] == jnp.arange(modes)[None, None, :]

    def pick(values):
        return jnp.sum(jnp.where(mode_hot, values, 0.0), -1)

    live = (flag >= 0).astype(F32)
    weight = jnp.sqrt(1.0 + pick(levels.astype(F32)[:, None, :])) * live
    real = pick(coupling[0][None, None, :]) * weight
    imag = pick(coupling[1][None, None, :]) * weight
    other = jnp.where(flag == 1, imag, -imag)
    op_hot = mode[:, :, None] % 3 == jnp.arange(3)[None, None, :]
    slot_hot = slot[:, :, None] == jnp.arange(slots)[None, None, :]
    both = op_hot[:, :, :, None] & slot_hot[:, :, None, :]

    def spread(values):
        return jnp.sum(jnp.where(both, values[:, :, None, None], 0.0), 1)

    creal, left, right = spread(real), spread(imag), spread(other)

    def parts(cimag):
        return jnp.stack([jnp.stack([creal, -cimag], -1), jnp.stack([cimag, creal], -1)], 1)

    table = jnp.stack([parts(left), parts(right)], 1)
    table = table.reshape(-1, slots * 2)
    high = lax.reduce_precision(table, 8, 7)
    table_high, table_low = high.astype(BF16), (table - high).astype(BF16)
    pair = mode_hot[:, :, :, None] & slot_hot[:, :, None, :]
    corr = jnp.sum(jnp.where(pair, weight[:, :, None, None], 0.0), 1)
    return table_high, table_low, corr


def blown_up(table):
    tall, wide = table.shape
    down = (jnp.arange(tall * ROWS)[:, None] // ROWS == jnp.arange(tall)[None, :]).astype(BF16)
    along = (jnp.arange(wide)[:, None] == jnp.arange(wide * ROWS)[None, :] // ROWS).astype(BF16)
    big = jnp.dot(down, table, preferred_element_type=F32).astype(BF16)
    big = jnp.dot(big, along, preferred_element_type=F32)
    keep = jnp.arange(tall * ROWS)[:, None] % ROWS == jnp.arange(wide * ROWS)[None, :] % ROWS
    return jnp.where(keep, big, 0.0).astype(BF16)


def greet(devices):
    barrier = pltpu.get_barrier_semaphore()
    for device in devices:
        pl.semaphore_signal(barrier, inc=1, device_id=device, device_id_type=MESH)
    pl.semaphore_wait(barrier, len(devices))


def remote(source, target, send, landed, device):
    return pltpu.make_async_remote_copy(
        src_ref=source,
        dst_ref=target,
        send_sem=send,
        recv_sem=landed,
        device_id=device,
        device_id_type=MESH,
    )


def section_kernel(
    tiers,
    first,
    decay_ref,
    index_ref,
    index_hbm,
    coef_ref,
    state_ref,
    ops_ref,
    before_ref,
    out_ref,
    corr_ref,
    other_hbm,
    mixed,
    acc,
    near_out,
    near,
    far_out,
    far,
    other,
    index_sems,
    block_send,
    block_land,
    near_send,
    near_land,
    far_send,
    far_land,
    *blocks,
):
    count, _, width, _ = state_ref.shape
    half, cap = near.shape[:2]
    slots = 2 * half * cap
    piece = width // PIECES
    me, mat = lax.axis_index("tier"), lax.axis_index("mat")
    base = me // half * half
    local = me - base
    peers = [lax.rem(local + d, half) for d in range(1, half)]
    partner = (lax.rem(me + half, tiers), mat)
    greet([(base + peer, mat) for peer in peers] + [partner])

    def span(k):
        return pl.ds(k * piece, piece)

    index_copy = remote(index_hbm, other_hbm, index_sems.at[0], index_sems.at[1], partner)
    index_copy.start()
    block_copies = [
        remote(
            state_ref.at[:, :, span(k), :],
            blocks[k],
            block_send.at[k],
            block_land.at[k],
            partner,
        )
        for k in range(PIECES)
    ]
    for copy in block_copies:
        copy.start()

    def to_peers(source, target, send, land, k):
        return [
            remote(
                source.at[peer, :, :, span(k), :],
                target.at[local, :, :, span(k), :],
                send.at[k, d],
                land.at[k, d],
                (base + peer, mat),
            )
            for d, peer in enumerate(peers)
        ]

    near_copies = [to_peers(near_out, near, near_send, near_land, k) for k in range(PIECES)]
    far_copies = [to_peers(far_out, far, far_send, far_land, k) for k in range(PIECES)]

    @pl.loop(0, half)
    def _(peer):
        for s in range(cap):
            near_out[peer, s] = state_ref[index_ref[0, (base + peer) * cap + s]]

    for copy in near_copies[0]:
        copy.start()
    for s in range(cap):
        near[local, s] = state_ref[index_ref[0, me * cap + s]]
    corr_ref[...] = before_ref[...]

    @pl.loop(0, count)
    def _(n):
        for part in range(2):
            turned = -state_ref[n, 1] if part == 0 else state_ref[n, 0]
            rate = jnp.dot(ops_ref[0], turned, preferred_element_type=F32)
            rate -= jnp.dot(turned, ops_ref[0], preferred_element_type=F32)
            acc[n, part] = rate - decay_ref[n] * state_ref[n, part].astype(F32)

    index_copy.wait()
    load_index = pltpu.make_async_copy(other_hbm, other, index_sems.at[2])
    load_index.start()
    load_index.wait()

    def forward(k):
        block_copies[k].wait_recv()

        @pl.loop(0, half)
        def _(peer):
            for s in range(cap):
                far_out[peer, s, :, span(k), :] = blocks[k][other[0, (base + peer) * cap + s]]

        for copy in far_copies[k]:
            copy.start()
        for s in range(cap):
            far[local, s, :, span(k), :] = blocks[k][other[0, me * cap + s]]

    def combine(k):
        for copy in near_copies[k] + far_copies[k]:
            copy.wait_recv()

        @pl.loop(0, piece // ROWS)
        def _(step):
            rows = pl.ds(pl.multiple_of(k * piece + step * ROWS, ROWS), ROWS)
            chunk = jnp.concatenate(
                [
                    near[:, :, :, rows, :].reshape(half * cap, 2, ROWS, width),
                    far[:, :, :, rows, :].reshape(half * cap, 2, ROWS, width),
                ],
                0,
            )
            tall = chunk.reshape(slots * 2 * ROWS, width)
            sums = jnp.dot(coef_ref[0], tall, preferred_element_type=F32)
            sums += jnp.dot(coef_ref[1], tall, preferred_element_type=F32)
            mixed[:, :, :, :, rows, :] = sums.astype(BF16).reshape(count, 2, 2, 3, ROWS, width)
            for part in range(2):
                corr_ref[...] += lax.dot_general(
                    state_ref[:, part, rows, :].reshape(count * ROWS, width),
                    chunk[:, part].reshape(slots * ROWS, width),
                    (((1,), (1,)), ((), ())),
                    preferred_element_type=F32,
                )

        for n in range(count):
            back = 0.0
            for q in range(3):
                right = mixed[n, 1, :, q, span(k), :].reshape(2 * piece, width)
                back += jnp.dot(right, ops_ref[1 + q], preferred_element_type=F32)
            acc[n, :, span(k), :] -= back.reshape(2, piece, width)

    for k in range(PIECES + 1):
        if k < PIECES:
            forward(k)
        if k + 1 < PIECES:
            for copy in near_copies[k + 1]:
                copy.start()
        if k > 0:
            combine(k - 1)

    @pl.loop(0, count)
    def _(n):
        for part in range(2):
            rate = acc[n, part]
            for q in range(3):
                rate += jnp.dot(ops_ref[1 + q], mixed[n, 0, part, q], preferred_element_type=F32)
            if first:
                out_ref[n, part] = (state_ref[n, part].astype(F32) + 0.125 * rate).astype(BF16)
            else:
                out_ref[n, part] = 0.25 * rate

    for k in range(PIECES):
        for copy in [block_copies[k]] + near_copies[k] + far_copies[k]:
            copy.wait_send()


def section(tiers, first, decay, index, coef, state, operators, before):
    count, _, width, _ = state.shape
    half, cap = tiers // 2, index.shape[1] // tiers
    vmem = pl.BlockSpec(memory_space=pltpu.VMEM)
    smem = pl.BlockSpec(memory_space=pltpu.SMEM)
    anywhere = pl.BlockSpec(memory_space=pl.ANY)
    slab = pltpu.VMEM((half, cap) + state.shape[1:], BF16)
    dma = pltpu.SemaphoreType.DMA
    return pl.pallas_call(
        functools.partial(section_kernel, tiers, first),
        out_shape=(
            jax.ShapeDtypeStruct(state.shape, BF16 if first else F32),
            jax.ShapeDtypeStruct(before.shape, F32),
            jax.ShapeDtypeStruct(index.shape, index.dtype),
        ),
        in_specs=[smem, smem, anywhere, vmem, vmem, vmem, vmem],
        out_specs=(vmem, vmem, anywhere),
        scratch_shapes=[
            pltpu.VMEM((count, 2, 2, 3, width, width), BF16),
            pltpu.VMEM(state.shape, F32),
            slab,
            slab,
            slab,
            slab,
            pltpu.SMEM(index.shape, index.dtype),
            dma((3,)),
            dma((PIECES,)),
            dma((PIECES,)),
        ]
        + [dma((PIECES, half - 1))] * 4
        + [pltpu.VMEM((count, 2, width // PIECES, width), BF16)] * PIECES,
        compiler_params=pltpu.CompilerParams(
            vmem_limit_bytes=56 << 20, collective_id=0 if first else 1, has_side_effects=True
        ),
        name="section_first" if first else "section_second",
    )(decay, index, index, coef, state, operators, before)


def total_kernel(tiers, mats, value_ref, total_ref, by_tier, by_mat, middle, send, landed, send_mat, landed_mat):
    me, mat = lax.axis_index("tier"), lax.axis_index("mat")
    along = [(lax.rem(me + d, tiers), mat) for d in range(1, tiers)]
    across = [(me, lax.rem(mat + d, mats)) for d in range(1, mats)]
    greet(along + across)
    copies = [
        remote(value_ref, by_tier.at[me], send.at[d], landed.at[d], device)
        for d, device in enumerate(along)
    ]
    for copy in copies:
        copy.start()
    by_tier[me] = value_ref[...]
    for copy in copies:
        copy.wait()
    middle[...] = jnp.sum(by_tier[...], 0)
    by_mat[mat] = middle[...]
    copies = [
        remote(middle, by_mat.at[mat], send_mat.at[d], landed_mat.at[d], device)
        for d, device in enumerate(across)
    ]
    for copy in copies:
        copy.start()
    for copy in copies:
        copy.wait()
    total_ref[...] = jnp.sum(by_mat[...], 0)


def total(tiers, mats, number, value):
    vmem = pl.BlockSpec(memory_space=pltpu.VMEM)
    return pl.pallas_call(
        functools.partial(total_kernel, tiers, mats),
        out_shape=jax.ShapeDtypeStruct(value.shape, F32),
        in_specs=[vmem],
        out_specs=vmem,
        scratch_shapes=[
            pltpu.VMEM((tiers,) + value.shape, F32),
            pltpu.VMEM((mats,) + value.shape, F32),
            pltpu.VMEM(value.shape, F32),
            pltpu.SemaphoreType.DMA((tiers - 1,)),
            pltpu.SemaphoreType.DMA((tiers - 1,)),
            pltpu.SemaphoreType.DMA((mats - 1,)),
            pltpu.SemaphoreType.DMA((mats - 1,)),
        ],
        compiler_params=pltpu.CompilerParams(collective_id=number, has_side_effects=True),
        name="total",
    )(value)


def per_device(
    tiers,
    mats,
    costate,
    hamiltonian,
    couplers,
    damping,
    coupling,
    levels,
    neighbour_slot,
    neighbour_mode,
    neighbour_flag,
    send_index,
):
    count, _, width, _ = costate.shape
    slots = send_index.shape[1]
    half, cap = tiers // 2, slots // tiers
    me = lax.axis_index("tier")
    base = me // half * half

    operators = jnp.concatenate([symmetric(hamiltonian)[None], symmetric(couplers)], 0)
    nearest = (neighbour_slot + base * cap) % slots
    table_high, table_low, corr_weight = coefficients(
        coupling, levels, nearest, neighbour_mode, neighbour_flag, slots
    )
    coef = jnp.stack([blown_up(table_high), blown_up(table_low)])
    decay = jnp.sum(levels.astype(F32) * damping[None, :], 1)
    corr = jnp.zeros((count * ROWS, slots * ROWS), F32)
    middle, corr, _ = section(tiers, True, decay, send_index, coef, costate, operators, corr)
    increment, corr, _ = section(tiers, False, decay, send_index, coef, middle, operators, corr)
    row = jnp.arange(count * ROWS)[:, None]
    column = jnp.arange(slots * ROWS)[None, :]
    corr = jnp.where(row % ROWS == column % ROWS, corr, 0.0)
    pairs = jnp.sum(corr.reshape(count, ROWS, slots, ROWS), (1, 3)) / width
    grads = jnp.sum(pairs[:, None, :] * corr_weight, (0, 2))
    modes = grads.shape[0]
    padded = jnp.zeros((8, 128), F32).at[0, :modes].set(grads)
    return increment, total(tiers, mats, 2, padded)[0, :modes]


def solution(mesh):
    blocks = P(("tier", "mat"), None)
    return jax.shard_map(
        functools.partial(per_device, mesh.shape["tier"], mesh.shape["mat"]),
        mesh=mesh,
        in_specs=(P(("tier", "mat"), None, None, None), P(), P(), P(), P()) + (blocks,) * 5,
        out_specs=(P(("tier", "mat"), None, None, None), P()),
        check_vma=False,
    )
```

time: 219 us -> 194 us (0.89)
  Pallas kernels: 194 us -> 174 us
  local copies, waits for them, and re-layouts: 18.8 us -> 8.3 us
  other arithmetic: 3.97 us -> 8.75 us
    pallas_call x6 -> x2, Pallas kernels: 183 us -> 161 us  [section(): pl.pallas_call(functools.partial(section_kernel, tiers, first), out_shape...]
    gather x4 -> x0, local copies, waits for them, and re-layouts: 11.7 us -> none  [chosen(): return state[mine].reshape((half, cap) + state.shape[1:])]
where the time goes in v2:
time: 194 us
  Pallas kernels  174 us (90%)
  other arithmetic  8.75 us (5%)
  local copies, waits for them, and re-layouts  8.3 us (4%)
    pallas_call x2, Pallas kernels, section(): pl.pallas_call(functools.partial(section_kernel, tiers, first), out_shape...  161 us
    pallas_call x1, Pallas kernels, total(): pl.pallas_call(functools.partial(total_kernel, tiers, mats), out_shape=ja...  13.1 us

profile of v2, /device:TPU:0, one launch (start us, length us, event | category | flops | bytes accessed | tf_op | source)
XLA Modules:
  0.0 193.6 jit_solution(2110946475637034517)
XLA Ops:
  0.6 0.7 add_select_fusion.3
  1.4 0.8 slice_bitcast_fusion.2
  2.1 0.7 convert_element_type.39
  2.8 0.1 copy.27
  2.9 0.8 select_reduce_fusion.1
  3.7 0.7 fusion.36
  4.4 0.7 negate_select_fusion
  5.1 0.7 add_select_fusion.4
  5.8 0.2 fusion.14
  6.1 0.4 copy.36
  6.5 0.4 reshape.217
  6.9 0.6 fusion.3
  7.5 0.6 fusion.2
  8.2 0.0 copy-start
  8.2 1.3 pad_maximum_fusion.coef_ref
  9.5 0.0 copy-done
  9.5 0.0 copy-start.1
  9.5 0.2 copy.39
  9.7 0.2 copy.40
  9.8 0.0 copy-start.3
  9.9 0.0 copy-start.4
  9.9 0.1 fusion.5
  10.0 0.4 copy-done.1
  10.4 0.1 copy.37
  10.5 0.1 copy.38
  10.6 0.8 pad_maximum_fusion.1.ops_ref
  11.5 0.0 copy-done.3
  11.5 0.0 copy-done.4
  11.5 0.6 multiply_reduce_fusion.1.decay_ref
  12.1 0.6 broadcast_in_dim.125.before_ref
  12.7 81.6 %section_first.1 = (bf16[4,2,256,256]{3,2,1,0:T(8,128)(2,1)}, f32[64,256]{1,0:T(8,128)}, s32[1,16]{1,0:T(1,128)}) custom-call(f32[4]{0:T(128)} %multiply_reduce_fusion.1.decay_ref, s32[1,16]{1,0:T(1,128)} %index_hbm.3, s32[1,16]{1,0:T(1,128)} %index_hbm.3, bf16[2,768,512]{2,1,0:T(8,128)(2,1)} %pad_maximum_fusion.coef_ref, ...), custom_call_target="tpu_custom_call" | custom-call | tf_op jit(solution)/shard_map/section_first/pallas_call | solution.py:259
  94.4 0.0 copy-start.2
  94.4 79.6 %section_second.1 = (f32[4,2,256,256]{3,2,1,0:T(8,128)}, f32[64,256]{1,0:T(8,128)}, s32[1,16]{1,0:T(1,128)}) custom-call(f32[4]{0:T(128)} %multiply_reduce_fusion.1.decay_ref, s32[1,16]{1,0:T(1,128)} %index_hbm.3, s32[1,16]{1,0:T(1,128)} %index_hbm.3, bf16[2,768,512]{2,1,0:T(8,128)(2,1)} %pad_maximum_fusion.coef_ref, ...), custom_call_target="tpu_custom_call" | custom-call | tf_op jit(solution)/shard_map/section_second/pallas_call | solution.py:259
  174.0 0.9 compare_select_fusion.2
  174.9 0.2 reshape.218
  175.1 0.1 reduce_sum.103
  175.2 0.0 copy-done.2
  175.3 0.2 select_reduce_fusion
  175.4 0.1 multiply_reduce_fusion
  175.6 0.6 scatter.4.value_ref
  176.2 13.1 %total.1 = f32[8,128]{1,0:T(8,128)} custom-call(f32[8,128]{1,0:T(8,128)} %scatter.4.value_ref), custom_call_target="tpu_custom_call" | custom-call | tf_op jit(solution)/shard_map/total/pallas_call | solution.py:318
  189.3 1.2 slice_bitcast_fusion
  190.5 3.0 %copy.45 = f32[4,2,256,256]{3,2,1,0:T(8,128)} copy(f32[4,2,256,256]{3,2,1,0:T(8,128)} %get-tuple-element.46) | data formatting | bytes 4194304
  (20 shorter events, 0.2 us)
Async XLA Ops:
  8.2 1.3 copy-start
  9.5 0.9 copy-start.1
  9.8 1.6 copy-start.3
  9.9 1.6 copy-start.4
  94.4 80.9 %copy-start.2 = (s32[4,24]{1,0:T(4,128)S(1)}, s32[4,24]{1,0:T(4,128)}, u32[]{:S(2)}) copy-start(s32[4,24]{1,0:T(4,128)} %param.19) | copy-start | bytes 1156

commit v3 on v2

--- a/solution.py
+++ b/solution.py
@@ -8,7 +8,7 @@
 from jax.sharding import PartitionSpec as P
 
 ROWS = 16
-PIECES = 4
+PIECES = 8
 F32 = jnp.float32
 BF16 = jnp.bfloat16
 MESH = pl.DeviceIdType.MESH
@@ -52,14 +52,26 @@
     return table_high, table_low, corr
 
 
-def blown_up(table):
-    tall, wide = table.shape
-    down = (jnp.arange(tall * ROWS)[:, None] // ROWS == jnp.arange(tall)[None, :]).astype(BF16)
-    along = (jnp.arange(wide)[:, None] == jnp.arange(wide * ROWS)[None, :] // ROWS).astype(BF16)
-    big = jnp.dot(down, table, preferred_element_type=F32).astype(BF16)
-    big = jnp.dot(big, along, preferred_element_type=F32)
-    keep = jnp.arange(tall * ROWS)[:, None] % ROWS == jnp.arange(wide * ROWS)[None, :] % ROWS
-    return jnp.where(keep, big, 0.0).astype(BF16)
+def blow_up(table_ref, coef_ref):
+    _, tall, wide = table_ref.shape
+    bits = ROWS.bit_length() - 1
+
+    def iota(shape, axis):
+        return lax.broadcasted_iota(jnp.int32, shape, axis)
+
+    def hot(keep):
+        return jnp.where(keep, 1.0, 0.0).astype(BF16)
+
+    shape = (tall * ROWS, tall)
+    down = hot(iota(shape, 0) >> bits == iota(shape, 1))
+    shape = (wide, wide * ROWS)
+    along = hot(iota(shape, 0) == iota(shape, 1) >> bits)
+    shape = (tall * ROWS, wide * ROWS)
+    keep = iota(shape, 0) & (ROWS - 1) == iota(shape, 1) & (ROWS - 1)
+    for half in range(2):
+        big = jnp.dot(down, table_ref[half], preferred_element_type=F32).astype(BF16)
+        big = jnp.dot(big, along, preferred_element_type=F32)
+        coef_ref[half] = jnp.where(keep, big, 0.0).astype(BF16)
 
 
 def greet(devices):
@@ -86,13 +98,14 @@
     decay_ref,
     index_ref,
     index_hbm,
-    coef_ref,
+    table_ref,
     state_ref,
     ops_ref,
     before_ref,
     out_ref,
     corr_ref,
     other_hbm,
+    coef_ref,
     mixed,
     acc,
     near_out,
@@ -162,7 +175,8 @@
         copy.start()
     for s in range(cap):
         near[local, s] = state_ref[index_ref[0, me * cap + s]]
-    corr_ref[...] = before_ref[...]
+    corr_ref[...] = jnp.zeros_like(corr_ref) if first else before_ref[...]
+    blow_up(table_ref, coef_ref)
 
     @pl.loop(0, count)
     def _(n):
@@ -266,6 +280,7 @@
         in_specs=[smem, smem, anywhere, vmem, vmem, vmem, vmem],
         out_specs=(vmem, vmem, anywhere),
         scratch_shapes=[
+            pltpu.VMEM((2, coef.shape[1] * ROWS, coef.shape[2] * ROWS), BF16),
             pltpu.VMEM((count, 2, 2, 3, width, width), BF16),
             pltpu.VMEM(state.shape, F32),
             slab,
@@ -359,7 +374,7 @@
     table_high, table_low, corr_weight = coefficients(
         coupling, levels, nearest, neighbour_mode, neighbour_flag, slots
     )
-    coef = jnp.stack([blown_up(table_high), blown_up(table_low)])
+    coef = jnp.stack([table_high, table_low])
     decay = jnp.sum(levels.astype(F32) * damping[None, :], 1)
     corr = jnp.zeros((count * ROWS, slots * ROWS), F32)
     middle, corr, _ = section(tiers, True, decay, send_index, coef, costate, operators, corr)

time: 194 us -> 206 us (1.062)
  Pallas kernels: 174 us -> 187 us
    pallas_call x2, Pallas kernels: 161 us -> 175 us  [section(): pl.pallas_call(functools.partial(section_kernel, tiers, first), out_shape...]
    unnamed x13 -> x11, local copies, waits for them, and re-layouts: 3.76 us -> 4.33 us
where the time goes in v3:
time: 206 us; the launch traced here: 205 us
  Pallas kernels  187 us (91%)
  local copies, waits for them, and re-layouts  9.01 us (4%)
  other arithmetic  8.09 us (4%)
    pallas_call x2, Pallas kernels, section(): pl.pallas_call(functools.partial(section_kernel, tiers, first), out_shape...  175 us
    pallas_call x1, Pallas kernels, total(): pl.pallas_call(functools.partial(total_kernel, tiers, mats), out_shape=ja...  12.2 us
    unnamed x11, local copies, waits for them, and re-layouts  4.33 us

profile of v3, /device:TPU:0, one launch (start us, length us, event | category | flops | bytes accessed | tf_op | source)
XLA Modules:
  0.0 205.3 jit_solution(4206373128017062786)
XLA Ops:
  0.6 0.7 add_select_fusion
  1.4 0.8 slice_bitcast_fusion.2
  2.1 0.7 convert_element_type.37
  2.8 0.1 copy.38
  2.9 0.8 select_reduce_fusion.1
  3.7 0.7 fusion.15
  4.4 0.7 negate_select_fusion
  5.1 0.7 add_select_fusion.1
  5.8 0.2 fusion.6
  6.1 0.4 copy.42
  6.5 0.0 copy-start
  6.5 0.4 reshape.142
  6.9 0.1 copy.43
  6.9 0.1 copy.44
  7.0 0.6 pad_maximum_fusion.2.table_ref
  7.6 1.2 copy.48
  8.8 0.2 copy.49
  9.0 0.0 copy-start.2
  9.0 0.0 copy-start.3
  9.0 0.1 fusion.1
  9.1 0.0 copy-done
  9.1 0.1 copy.46
  9.2 0.1 copy.47
  9.4 0.8 pad_maximum_fusion.ops_ref
  10.2 0.0 copy-done.2
  10.2 0.0 copy-done.3
  10.2 0.6 multiply_reduce_fusion.1.decay_ref
  10.9 0.6 broadcast_in_dim.107.before_ref
  11.5 0.0 copy-start.1
  11.5 88.5 %section_first.1 = (bf16[4,2,256,256]{3,2,1,0:T(8,128)(2,1)}, f32[64,256]{1,0:T(8,128)}, s32[1,16]{1,0:T(1,128)}) custom-call(f32[4]{0:T(128)} %multiply_reduce_fusion.1.decay_ref, s32[1,16]{1,0:T(1,128)} %index_hbm.3, s32[1,16]{1,0:T(1,128)} %index_hbm.3, bf16[2,48,32]{2,1,0:T(8,128)(2,1)} %pad_maximum_fusion.2.table_ref, ...), custom_call_target="tpu_custom_call" | custom-call | tf_op jit(solution)/shard_map/section_first/pallas_call | solution.py:273
  100.0 86.6 %section_second.1 = (f32[4,2,256,256]{3,2,1,0:T(8,128)}, f32[64,256]{1,0:T(8,128)}, s32[1,16]{1,0:T(1,128)}) custom-call(f32[4]{0:T(128)} %multiply_reduce_fusion.1.decay_ref, s32[1,16]{1,0:T(1,128)} %index_hbm.3, s32[1,16]{1,0:T(1,128)} %index_hbm.3, bf16[2,48,32]{2,1,0:T(8,128)(2,1)} %pad_maximum_fusion.2.table_ref, ...), custom_call_target="tpu_custom_call" | custom-call | tf_op jit(solution)/shard_map/section_second/pallas_call | solution.py:273
  186.6 0.9 compare_select_fusion
  187.6 0.2 reshape.143
  187.8 0.1 reduce_sum.103
  187.9 0.0 copy-done.1
  187.9 0.2 select_reduce_fusion
  188.1 0.1 multiply_reduce_fusion
  188.2 0.6 scatter.4.value_ref
  188.8 12.2 %total.1 = f32[8,128]{1,0:T(8,128)} custom-call(f32[8,128]{1,0:T(8,128)} %scatter.4.value_ref), custom_call_target="tpu_custom_call" | custom-call | tf_op jit(solution)/shard_map/total/pallas_call | solution.py:333
  201.0 1.2 slice_bitcast_fusion
  202.2 3.0 %copy.60 = f32[4,2,256,256]{3,2,1,0:T(8,128)} copy(f32[4,2,256,256]{3,2,1,0:T(8,128)} %get-tuple-element.48) | data formatting | bytes 4194304
  (16 shorter events, 0.2 us)
Async XLA Ops:
  6.5 2.6 %copy-start = (bf16[256,256]{1,0:T(8,128)(2,1)S(1)}, bf16[256,256]{1,0:T(8,128)(2,1)}, u32[]{:S(2)}) copy-start(bf16[256,256]{1,0:T(8,128)(2,1)} %param.13) | copy-start | bytes 393220
  9.0 1.2 copy-start.2
  9.0 1.2 copy-start.3
  11.5 176.4 %copy-start.1 = (s32[4,24]{1,0:T(4,128)S(1)}, s32[4,24]{1,0:T(4,128)}, u32[]{:S(2)}) copy-start(s32[4,24]{1,0:T(4,128)} %param.19) | copy-start | bytes 1156

commit v4 on v2

--- a/solution.py
+++ b/solution.py
@@ -8,7 +8,7 @@
 from jax.sharding import PartitionSpec as P
 
 ROWS = 16
-PIECES = 4
+PIECES = 2
 F32 = jnp.float32
 BF16 = jnp.bfloat16
 MESH = pl.DeviceIdType.MESH

time: 194 us -> 199 us (1.026)
  Pallas kernels: 174 us -> 179 us
    pallas_call x2, Pallas kernels: 161 us -> 165 us  [section(): pl.pallas_call(functools.partial(section_kernel, tiers, first), out_shape...]
where the time goes in v4:
time: 199 us; the launch traced here: 198 us
  Pallas kernels  179 us (90%)
  other arithmetic  8.75 us (4%)
  local copies, waits for them, and re-layouts  8.3 us (4%)
    pallas_call x2, Pallas kernels, section(): pl.pallas_call(functools.partial(section_kernel, tiers, first), out_shape...  165 us
    pallas_call x1, Pallas kernels, total(): pl.pallas_call(functools.partial(total_kernel, tiers, mats), out_shape=ja...  14.4 us

profile of v4, /device:TPU:0, one launch (start us, length us, event | category | flops | bytes accessed | tf_op | source)
XLA Modules:
  0.0 198.2 jit_solution(938314291749663607)
XLA Ops:
  0.6 0.7 add_select_fusion.3
  1.4 0.8 slice_bitcast_fusion.2
  2.1 0.7 convert_element_type.39
  2.8 0.1 copy.27
  2.9 0.8 select_reduce_fusion.1
  3.7 0.7 fusion.36
  4.4 0.7 negate_select_fusion
  5.1 0.7 add_select_fusion.4
  5.8 0.2 fusion.14
  6.1 0.4 copy.36
  6.5 0.4 reshape.217
  6.9 0.6 fusion.3
  7.5 0.6 fusion.2
  8.2 0.0 copy-start
  8.2 1.3 pad_maximum_fusion.coef_ref
  9.5 0.0 copy-done
  9.5 0.0 copy-start.1
  9.5 0.2 copy.39
  9.7 0.2 copy.40
  9.8 0.0 copy-start.3
  9.9 0.0 copy-start.4
  9.9 0.1 fusion.5
  10.0 0.4 copy-done.1
  10.4 0.1 copy.37
  10.5 0.1 copy.38
  10.6 0.8 pad_maximum_fusion.1.ops_ref
  11.5 0.0 copy-done.3
  11.5 0.0 copy-done.4
  11.5 0.6 multiply_reduce_fusion.1.decay_ref
  12.1 0.6 broadcast_in_dim.125.before_ref
  12.7 82.6 %section_first.1 = (bf16[4,2,256,256]{3,2,1,0:T(8,128)(2,1)}, f32[64,256]{1,0:T(8,128)}, s32[1,16]{1,0:T(1,128)}) custom-call(f32[4]{0:T(128)} %multiply_reduce_fusion.1.decay_ref, s32[1,16]{1,0:T(1,128)} %index_hbm.3, s32[1,16]{1,0:T(1,128)} %index_hbm.3, bf16[2,768,512]{2,1,0:T(8,128)(2,1)} %pad_maximum_fusion.coef_ref, ...), custom_call_target="tpu_custom_call" | custom-call | tf_op jit(solution)/shard_map/section_first/pallas_call | solution.py:259
  95.3 0.0 copy-start.2
  95.3 82.0 %section_second.1 = (f32[4,2,256,256]{3,2,1,0:T(8,128)}, f32[64,256]{1,0:T(8,128)}, s32[1,16]{1,0:T(1,128)}) custom-call(f32[4]{0:T(128)} %multiply_reduce_fusion.1.decay_ref, s32[1,16]{1,0:T(1,128)} %index_hbm.3, s32[1,16]{1,0:T(1,128)} %index_hbm.3, bf16[2,768,512]{2,1,0:T(8,128)(2,1)} %pad_maximum_fusion.coef_ref, ...), custom_call_target="tpu_custom_call" | custom-call | tf_op jit(solution)/shard_map/section_second/pallas_call | solution.py:259
  177.4 0.9 compare_select_fusion.2
  178.3 0.2 reshape.218
  178.5 0.1 reduce_sum.103
  178.6 0.0 copy-done.2
  178.7 0.2 select_reduce_fusion
  178.8 0.1 multiply_reduce_fusion
  179.0 0.6 scatter.4.value_ref
  179.6 14.4 %total.1 = f32[8,128]{1,0:T(8,128)} custom-call(f32[8,128]{1,0:T(8,128)} %scatter.4.value_ref), custom_call_target="tpu_custom_call" | custom-call | tf_op jit(solution)/shard_map/total/pallas_call | solution.py:318
  193.9 1.2 slice_bitcast_fusion
  195.1 3.0 %copy.45 = f32[4,2,256,256]{3,2,1,0:T(8,128)} copy(f32[4,2,256,256]{3,2,1,0:T(8,128)} %get-tuple-element.46) | data formatting | bytes 4194304
  (20 shorter events, 0.2 us)
Async XLA Ops:
  8.2 1.3 copy-start
  9.5 0.9 copy-start.1
  9.8 1.6 copy-start.3
  9.9 1.6 copy-start.4
  95.3 83.3 %copy-start.2 = (s32[4,24]{1,0:T(4,128)S(1)}, s32[4,24]{1,0:T(4,128)}, u32[]{:S(2)}) copy-start(s32[4,24]{1,0:T(4,128)} %param.19) | copy-start | bytes 1156
